TPU v7x, 32 devices: a whole 2x2x4 slice. The times are simulated.
32 devices in a mesh: wide: 8 (over y, x, core), narrow: 4 (over z).
Axes of the slice: x: 2, y: 2, z: 4, core: 2. Of those that a mesh axis runs over, the one named last changes fastest.
Arguments:
- tokens: bfloat16 [64, 128, 1120], P(('wide', 'narrow')), may hold values from -6 to 6
- lengths: int32 [64], P(('wide', 'narrow')), may hold values from 1 to 128, 5120 in all
- ln1_gain: bfloat16 [1120], P('narrow'), may hold values from 0.5 to 1.5
- ln1_bias: bfloat16 [1120], P('narrow'), may hold values from -1 to 1
- w_qkv: bfloat16 [1120, 3360], P('narrow'), may hold values from -0.1875 to 0.1875
- w_out: bfloat16 [1120, 1120], P('narrow'), may hold values from -0.5 to 0.5
- ln2_gain: bfloat16 [1120], P('narrow'), may hold values from 0.5 to 1.5
- ln2_bias: bfloat16 [1120], P('narrow'), may hold values from -1 to 1
- w_fc: bfloat16 [1120, 4480], P('narrow'), may hold values from -0.1875 to 0.1875
- w_proj: bfloat16 [4480, 1120], P('narrow'), may hold values from -0.09375 to 0.09375
- cotangent: bfloat16 [64, 128, 1120], P(('wide', 'narrow')), may hold values from -6 to 6
Outputs:
- result: bfloat16 [64, 128, 1120], P(('wide', 'narrow'))
- grad_tokens: bfloat16 [64, 128, 1120], P(('wide', 'narrow'))
- grad_ln1_gain: float32 [1120], P('narrow')
- grad_ln1_bias: float32 [1120], P('narrow')
- grad_w_qkv: float32 [1120, 3360], P('narrow')
- grad_w_out: float32 [1120, 1120], P('narrow')
- grad_ln2_gain: float32 [1120], P('narrow')
- grad_ln2_bias: float32 [1120], P('narrow')
- grad_w_fc: float32 [1120, 4480], P('narrow')
- grad_w_proj: float32 [4480, 1120], P('narrow')
All inputs are finite; a program needn't handle non-finite values. No bound on the sum of `lengths` on one device may be relied on, other than what follows from the above.
Results may differ from a plain program's by a relative error of at most 0.015.
Values may be sent and summed in bfloat16 or wider, within the bound.
A program may use at most 256 MiB of HBM per device.

v0:
```python
from functools import partial
import jax
import jax.numpy as jnp
from jax import lax
from jax.sharding import PartitionSpec as P

HEADS = 20
EPS = 1e-05
MASKED = -1e30


def layer_norm(in_rows, gain_vec, shift_vec):
    row_mean = jnp.mean(in_rows, axis=-1, keepdims=True)
    centered = in_rows - row_mean
    inv_std = lax.rsqrt(jnp.mean(centered * centered, axis=-1, keepdims=True) + EPS)
    normed = centered * inv_std
    return (normed * gain_vec + shift_vec, normed, inv_std)


def norm_grad(grad_rows, gain_vec, normed, inv_std):
    scaled = grad_rows * gain_vec
    return inv_std * (
        scaled
        - jnp.mean(scaled, axis=-1, keepdims=True)
        - normed * jnp.mean(scaled * normed, axis=-1, keepdims=True)
    )


def inner_rows(left, right):
    return lax.dot_general(
        left, right, (((0,), (0,)), ((), ())), preferred_element_type=jnp.float32
    )


def times_trans(left, right):
    return lax.dot_general(
        left, right, (((1,), (1,)), ((), ())), preferred_element_type=jnp.float32
    )


def attn_scores(queries, key_rows, length):
    seq_len = queries.shape[0]
    head_size = queries.shape[2]
    scores = jnp.einsum(
        "qhd,khd->hqk", queries, key_rows, preferred_element_type=jnp.float32
    ) * head_size ** (-0.5)
    query_pos = lax.broadcasted_iota(jnp.int32, (seq_len, seq_len), 0)
    key_pos = lax.broadcasted_iota(jnp.int32, (seq_len, seq_len), 1)
    allowed = (key_pos <= query_pos) & (key_pos < length)
    return jnp.where(allowed[None], scores, MASKED)


def forward_cell(in_rows, length, weights):
    gain_one, shift_one, weight_qkv, weight_out, gain_two, shift_two, weight_fc, weight_proj = (
        weights
    )
    seq_len, model_width = in_rows.shape
    head_size = model_width // HEADS
    first_norm, normed_one, inv_one = layer_norm(
        in_rows, gain_one.astype(jnp.float32), shift_one.astype(jnp.float32)
    )
    first_low = first_norm.astype(jnp.bfloat16)
    projected = jnp.dot(first_low, weight_qkv, preferred_element_type=jnp.float32)
    queries = projected[:, :model_width].astype(jnp.bfloat16).reshape(seq_len, HEADS, head_size)
    key_rows = (
        projected[:, model_width : 2 * model_width]
        .astype(jnp.bfloat16)
        .reshape(seq_len, HEADS, head_size)
    )
    value_rows = (
        projected[:, 2 * model_width :].astype(jnp.bfloat16).reshape(seq_len, HEADS, head_size)
    )
    scores = attn_scores(queries, key_rows, length)
    row_max = jnp.max(scores, axis=-1, keepdims=True)
    exp_scores = jnp.exp(scores - row_max)
    row_total = jnp.sum(exp_scores, axis=-1, keepdims=True)
    attn_prob = exp_scores / row_total
    log_total = row_max + jnp.log(row_total)
    heads_out = jnp.einsum(
        "hqk,khd->qhd",
        attn_prob.astype(jnp.bfloat16),
        value_rows,
        preferred_element_type=jnp.float32,
    )
    attended = heads_out.reshape(seq_len, model_width).astype(jnp.bfloat16)
    mixed_rows = in_rows + jnp.dot(attended, weight_out, preferred_element_type=jnp.float32)
    second_norm, normed_two, inv_two = layer_norm(
        mixed_rows, gain_two.astype(jnp.float32), shift_two.astype(jnp.float32)
    )
    second_low = second_norm.astype(jnp.bfloat16)
    pre_act = jnp.dot(second_low, weight_fc, preferred_element_type=jnp.float32)
    gelu_out = jax.nn.gelu(pre_act, approximate=True).astype(jnp.bfloat16)
    result = mixed_rows + jnp.dot(gelu_out, weight_proj, preferred_element_type=jnp.float32)
    saved_acts = (
        normed_one,
        inv_one,
        first_low,
        queries,
        key_rows,
        value_rows,
        log_total,
        attended,
        normed_two,
        inv_two,
        second_low,
        pre_act,
        gelu_out,
    )
    return (result, saved_acts)


def backward_cell(grad_rows, length, saved_acts, weights):
    gain_one, shift_one, weight_qkv, weight_out, gain_two, shift_two, weight_fc, weight_proj = (
        weights
    )
    (
        normed_one,
        inv_one,
        first_low,
        queries,
        key_rows,
        value_rows,
        log_total,
        attended,
        normed_two,
        inv_two,
        second_low,
        pre_act,
        gelu_out,
    ) = saved_acts
    seq_len, model_width = grad_rows.shape
    head_size = model_width // HEADS
    grad_low = grad_rows.astype(jnp.bfloat16)
    grad_wproj = inner_rows(gelu_out, grad_low)
    grad_gelu = times_trans(grad_low, weight_proj)
    unused, gelu_pull = jax.vjp(partial(jax.nn.gelu, approximate=True), pre_act)
    grad_pre = gelu_pull(grad_gelu)[0].astype(jnp.bfloat16)
    grad_wfc = inner_rows(second_low, grad_pre)
    grad_second = times_trans(grad_pre, weight_fc)
    grad_gain_two = jnp.sum(grad_second * normed_two, axis=0)
    grad_shift_two = jnp.sum(grad_second, axis=0)
    grad_mixed = grad_rows + norm_grad(
        grad_second, gain_two.astype(jnp.float32), normed_two, inv_two
    )
    mixed_low = grad_mixed.astype(jnp.bfloat16)
    grad_wout = inner_rows(attended, mixed_low)
    grad_attended = (
        times_trans(mixed_low, weight_out).astype(jnp.bfloat16).reshape(seq_len, HEADS, head_size)
    )
    scores = attn_scores(queries, key_rows, length)
    attn_prob = jnp.exp(scores - log_total)
    grad_value = jnp.einsum(
        "hqk,qhd->khd",
        attn_prob.astype(jnp.bfloat16),
        grad_attended,
        preferred_element_type=jnp.float32,
    )
    grad_prob = jnp.einsum(
        "qhd,khd->hqk", grad_attended, value_rows, preferred_element_type=jnp.float32
    )
    grad_scores = attn_prob * (grad_prob - jnp.sum(attn_prob * grad_prob, axis=-1, keepdims=True))
    grad_scores = grad_scores.astype(jnp.bfloat16)
    scale_factor = head_size ** (-0.5)
    grad_query = (
        jnp.einsum("hqk,khd->qhd", grad_scores, key_rows, preferred_element_type=jnp.float32)
        * scale_factor
    )
    grad_key = (
        jnp.einsum("hqk,qhd->khd", grad_scores, queries, preferred_element_type=jnp.float32)
        * scale_factor
    )
    grad_proj_in = jnp.concatenate(
        [
            grad_query.reshape(seq_len, model_width),
            grad_key.reshape(seq_len, model_width),
            grad_value.reshape(seq_len, model_width),
        ],
        axis=1,
    ).astype(jnp.bfloat16)
    grad_wqkv = inner_rows(first_low, grad_proj_in)
    grad_first = times_trans(grad_proj_in, weight_qkv)
    grad_gain_one = jnp.sum(grad_first * normed_one, axis=0)
    grad_shift_one = jnp.sum(grad_first, axis=0)
    grad_input = grad_mixed + norm_grad(
        grad_first, gain_one.astype(jnp.float32), normed_one, inv_one
    )
    grads = (
        grad_gain_one,
        grad_shift_one,
        grad_wqkv,
        grad_wout,
        grad_gain_two,
        grad_shift_two,
        grad_wfc,
        grad_wproj,
    )
    return (grads, grad_input)


def shards(
    tokens, lengths, ln1_gain, ln1_bias, w_qkv, w_out, ln2_gain, ln2_bias, w_fc, w_proj, cotangent
):
    outputs = []
    input_grads = []
    running = None
    held = None
    held = (
        lax.all_gather(ln1_gain, "narrow", axis=0, tiled=True),
        lax.all_gather(ln1_bias, "narrow", axis=0, tiled=True),
        lax.all_gather(w_qkv, "narrow", axis=0, tiled=True),
        lax.all_gather(w_out, "narrow", axis=0, tiled=True),
        lax.all_gather(ln2_gain, "narrow", axis=0, tiled=True),
        lax.all_gather(ln2_bias, "narrow", axis=0, tiled=True),
        lax.all_gather(w_fc, "narrow", axis=0, tiled=True),
        lax.all_gather(w_proj, "narrow", axis=0, tiled=True),
    )
    for micro_step in range(tokens.shape[0]):
        in_rows = tokens[micro_step].astype(jnp.float32)
        result, saved_acts = forward_cell(in_rows, lengths[micro_step], held)
        grads, grad_input = backward_cell(
            cotangent[micro_step].astype(jnp.float32), lengths[micro_step], saved_acts, held
        )
        running = grads if running is None else jax.tree.map(jnp.add, running, grads)
        outputs.append(result.astype(jnp.bfloat16))
        input_grads.append(grad_input.astype(jnp.bfloat16))
    totals = []
    for grad in running:
        part = lax.psum_scatter(
            grad.astype(jnp.bfloat16), "narrow", scatter_dimension=0, tiled=True
        )
        if part.ndim == 2:
            part = lax.psum(part, "wide").astype(jnp.float32)
        else:
            part = lax.psum(part.astype(jnp.float32), "wide")
        totals.append(part)
    return (
        jnp.stack(outputs),
        jnp.stack(input_grads),
        totals[0],
        totals[1],
        totals[2],
        totals[3],
        totals[4],
        totals[5],
        totals[6],
        totals[7],
    )


def solution(mesh):
    placed = (
        P(("wide", "narrow"), None, None),
        P(("wide", "narrow")),
        P("narrow"),
        P("narrow"),
        P("narrow", None),
        P("narrow", None),
        P("narrow"),
        P("narrow"),
        P("narrow", None),
        P("narrow", None),
        P(("wide", "narrow"), None, None),
    )
    return jax.shard_map(
        shards,
        mesh=mesh,
        in_specs=placed,
        out_specs=(
            P(("wide", "narrow"), None, None),
            P(("wide", "narrow"), None, None),
            P("narrow"),
            P("narrow"),
            P("narrow", None),
            P("narrow", None),
            P("narrow"),
            P("narrow"),
            P("narrow", None),
            P("narrow", None),
        ),
        check_vma=False,
    )
```

profile of v0, /device:TPU:0, one launch (start us, length us, event | category | flops | bytes accessed | tf_op | source)
XLA Modules:
  0.0 1292.5 jit_solution(16745767182800808506)
XLA Ops:
  12.4 21.1 %all-reduce.14 = (bf16[1120]{0:T(1024)(128)(2,1)S(1)}, bf16[1120]{0:T(1024)(128)(2,1)S(1)}, bf16[1120]{0:T(1024)(128)(2,1)S(1)}, bf16[1120]{0:T(1024)(128)(2,1)S(1)}) all-reduce(bf16[1120]{0:T(1024)(128)(2,1)S(1)} %dynamic-update-slice.1, bf16[1120]{0:T(1024)(128)(2,1)S(1)} %dynamic-update-slice, ...), channel_id=1, replica_groups=mesh['wide'=8,'narrow'=4] {'narrow'}, use_global_device_ids=true, to_apply=%add.1 | all-reduce | flops 4480 | bytes 17920
  36.0 115.5 %all-gather.5.cloned.1.call-done = bf16[1120,3360]{1,0:T(8,128)(2,1)} async-done(((bf16[280,3360]{1,0:T(8,128)(2,1)}), bf16[1120,3360]{1,0:T(8,128)(2,1)}) %all-gather.5.cloned.1.call-update) | async-done | bytes 7526416 | tf_op jit(solution)/shard_map/all_gather | solution.py:210
  151.5 6.6 convolution_convert_fusion.1
  160.1 45.3 %all-gather.7.cloned.1.call-done = bf16[1120,1120]{1,0:T(8,128)(2,1)} async-done(((bf16[280,1120]{1,0:T(8,128)(2,1)}), bf16[1120,1120]{1,0:T(8,128)(2,1)}) %all-gather.7.cloned.1.call-update) | async-done | bytes 2508816 | tf_op jit(solution)/shard_map/all_gather | solution.py:211
  205.3 2.8 fusion.113
  208.4 6.6 convolution_convert_fusion
  220.9 161.4 %all-gather.9.cloned.1.call-done = bf16[1120,4480]{1,0:T(8,128)(2,1)} async-done(((bf16[280,4480]{1,0:T(8,128)(2,1)}), bf16[1120,4480]{1,0:T(8,128)(2,1)}) %all-gather.9.cloned.1.call-update) | async-done | bytes 10035216 | tf_op jit(solution)/shard_map/all_gather | solution.py:214
  382.2 7.6 fusion.105
  389.9 173.2 %all-gather.11.cloned.1.call-done = bf16[4480,1120]{1,0:T(8,128)(2,1)} async-done(((bf16[1120,1120]{1,0:T(8,128)(2,1)}), bf16[4480,1120]{1,0:T(8,128)(2,1)}) %all-gather.11.cloned.1.call-update) | async-done | bytes 10035216 | tf_op jit(solution)/shard_map/all_gather | solution.py:215
  563.1 8.1 fusion.21
  572.3 2.8 fusion.114
  577.0 8.1 fusion.14
  585.1 3.9 multiply_reduce_fusion.3
  602.9 7.7 fusion.69
  610.7 8.7 fusion.2
  620.6 8.7 fusion.103
  629.4 11.7 fusion.1
  642.8 9.2 fusion.78
  652.0 14.9 %fusion = bf16[4480,1120]{1,0:T(8,128)(2,1)} fusion(f32[4480,1120]{1,0:T(8,128)} %fusion.78, bf16[2,128,1120]{1,2,0:T(8,128)(2,1)S(1)} %copy-done.38, f32[128,4480]{1,0:T(8,128)} %fusion.105), kind=kOutput, calls=%fused_computation.3 | convolution fusion | flops 1299701760 | bytes 32686080 | tf_op jit(solution)/shard_map/dot_general | solution.py:30
  670.7 5.7 fusion.68
  676.4 3.7 fusion.66
  680.1 21.4 %all-reduce.13 = (bf16[1120]{0:T(1024)(128)(2,1)S(1)}, bf16[1120]{0:T(1024)(128)(2,1)S(1)}, bf16[1120]{0:T(1024)(128)(2,1)S(1)}, bf16[1120]{0:T(1024)(128)(2,1)S(1)}) all-reduce(bf16[1120]{0:T(1024)(128)(2,1)S(1)} %add_convert_fusion.5, ...), channel_id=2, replica_groups=mesh['wide'=8,'narrow'=4] {'narrow'}, use_global_device_ids=true, to_apply=%region_24.25.clone | all-reduce | flops 4480 | bytes 17920
  701.6 78.5 %reduce-scatter.13.cloned.1.call-done = bf16[280,3360]{1,0:T(8,128)(2,1)} async-done(((bf16[1120,3360]{1,0:T(8,128)(2,1)}), bf16[280,3360]{1,0:T(8,128)(2,1)}) %reduce-scatter.13.cloned.1.call-update) | async-done | bytes 1881616
  780.2 187.7 %reduce-scatter.17.cloned.1.call-done = bf16[280,4480]{1,0:T(8,128)(2,1)} async-done(((bf16[1120,4480]{1,0:T(8,128)(2,1)}), bf16[280,4480]{1,0:T(8,128)(2,1)}) %reduce-scatter.17.cloned.1.call-update) | async-done | bytes 2508816
  967.8 182.3 %reduce-scatter.11.cloned.1.call-done = bf16[1120,1120]{1,0:T(8,128)(2,1)} async-done(((bf16[4480,1120]{1,0:T(8,128)(2,1)}), bf16[1120,1120]{1,0:T(8,128)(2,1)}) %reduce-scatter.11.cloned.1.call-update) | async-done | bytes 2508816 | tf_op jit(solution)/shard_map/reduce_scatter | solution.py:228
  1150.3 14.7 %all-reduce.11 = (f32[280]{0:T(512)}, f32[280]{0:T(512)}, f32[280]{0:T(512)}, f32[280]{0:T(512)}) all-reduce(f32[280]{0:T(512)S(1)} %dynamic-slice_convert_fusion.3, f32[280]{0:T(512)S(1)} %dynamic-slice_convert_fusion.2, f32[280]{0:T(512)S(1)} %dynamic-slice_convert_fusion.1, ...), channel_id=1, replica_groups=mesh['wide'=8,'narrow'=4] {'wide'}, use_global_device_ids=true, to_apply=%region_25.26 | all-reduce | flops 1120 | bytes 8960 | tf_op jit(solution)/shard_map/psum | solution.py:234
  1165.1 8.3 fusion.6
  1173.6 8.4 fusion.7
  1184.2 90.5 %all-reduce.17.cloned.1.call-done = (bf16[280,3360]{1,0:T(8,128)(2,1)}, bf16[280,1120]{1,0:T(8,128)(2,1)}, bf16[280,4480]{1,0:T(8,128)(2,1)}, bf16[1120,1120]{1,0:T(8,128)(2,1)}) async-done(((bf16[280,3360]{1,0:T(8,128)(2,1)}, bf16[280,1120]{1,0:T(8,128)(2,1)}, bf16[280,4480]{1,0:T(8,128)(2,1)}, bf16[1120,1120]{1,0:T(8,128)(2,1)}), (bf16[280,3360]{1,0:T(8,128)(2,1)}, bf16[280,1120]{1,0:T(8,128)(2,1)}, ...) | async-done | bytes 7526416 | tf_op jit(solution)/shard_map/psum | solution.py:232
  1274.7 2.4 convert_element_type.225
  1280.0 2.6 convert_element_type.231
  1282.8 2.7 convert_element_type.233
  (270 shorter events, 42.7 us)
Async XLA Ops:
  7.2 144.3 %all-gather.5.cloned.1.call-start = ((), (), s32[]{:S(2)}) async-start(), calls=%async_computation.4 | async-start | bytes 9676800 | tf_op jit(solution)/shard_map/all_gather | solution.py:210
  7.9 197.4 %all-gather.7.cloned.1.call-start = ((), (), s32[]{:S(2)}) async-start(), calls=%async_computation.5 | async-start | bytes 3225600 | tf_op jit(solution)/shard_map/all_gather | solution.py:211
  8.7 24.8 %copy-start.76 = (s32[2]{0:T(128)S(1)}, s32[2]{0:T(128)}, u32[]{:S(2)}) copy-start(s32[2]{0:T(128)} %param.12) | copy-start | bytes 28
  8.7 26.7 %copy-start.12 = (bf16[2,128,1120]{1,2,0:T(8,128)(2,1)S(1)}, bf16[2,128,1120]{1,2,0:T(8,128)(2,1)}, u32[]{:S(2)}) copy-start(bf16[2,128,1120]{1,2,0:T(8,128)(2,1)} %param.11) | copy-start | bytes 1720324
  8.7 373.5 %all-gather.9.cloned.1.call-start = ((), (), s32[]{:S(2)}) async-start(), calls=%async_computation.6 | async-start | bytes 12544000 | tf_op jit(solution)/shard_map/all_gather | solution.py:214
  9.5 553.6 %all-gather.11.cloned.1.call-start = ((), (), s32[]{:S(2)}) async-start(), calls=%async_computation.7 | async-start | bytes 12902400 | tf_op jit(solution)/shard_map/all_gather | solution.py:215
  10.0 691.6 %reduce-scatter.15.cloned.1.call-start = ((), (), s32[]{:S(2)}) async-start(), calls=%async_computation.10 | async-start | bytes 3225600
  35.6 172.8 %copy-start.67 = (f32[128]{0:T(128)}, f32[128]{0:T(128)S(1)}, u32[]{:S(2)}) copy-start(f32[128]{0:T(128)S(1)} %get-tuple-element.80) | copy-start | bytes 1540
  35.6 567.3 %copy-start.60 = (f32[128]{0:T(128)}, f32[128]{0:T(128)S(1)}, u32[]{:S(2)}) copy-start(f32[128]{0:T(128)S(1)} %get-tuple-element.81) | copy-start | bytes 1540
  35.8 567.1 %copy-start.63 = (f32[128]{0:T(128)}, f32[128]{0:T(128)S(1)}, u32[]{:S(2)}) copy-start(f32[128]{0:T(128)S(1)} %add_rsqrt_fusion.3) | copy-start | bytes 1540
  35.8 172.6 %copy-start.71 = (f32[128]{0:T(128)}, f32[128]{0:T(128)S(1)}, u32[]{:S(2)}) copy-start(f32[128]{0:T(128)S(1)} %add_rsqrt_fusion.1) | copy-start | bytes 1540
  160.1 48.1 %copy-start.53 = (bf16[20,56,128]{2,1,0:T(8,128)(2,1)}, bf16[20,56,128]{2,1,0:T(8,128)(2,1)S(1)}, u32[]{:S(2)}) copy-start(bf16[20,56,128]{2,1,0:T(8,128)(2,1)S(1)} %convolution_convert_fusion.7) | copy-start | bytes 860164
  208.2 411.3 %copy-start.6 = (f32[128,1120]{0,1:T(8,128)}, f32[128,1120]{0,1:T(8,128)S(1)}, u32[]{:S(2)}) copy-start(f32[128,1120]{0,1:T(8,128)S(1)} %get-tuple-element.73) | copy-start | bytes 1720324
  593.3 186.8 %reduce-scatter.13.cloned.1.call-start = ((), (), s32[]{:S(2)}) async-start(), calls=%async_computation.9 | async-start | bytes 9676800
  597.5 13.2 %copy-start.40 = (bf16[20,56,128]{2,1,0:T(8,128)(2,1)}, bf16[20,56,128]{2,1,0:T(8,128)(2,1)S(1)}, u32[]{:S(2)}) copy-start(bf16[20,56,128]{2,1,0:T(8,128)(2,1)S(1)} %fusion.27) | copy-start | bytes 860164
  597.8 12.9 copy-start.41
  619.4 10.0 copy-start.10
  619.4 348.4 %reduce-scatter.17.cloned.1.call-start = ((), (), s32[]{:S(2)}) async-start(), calls=%async_computation.11 | async-start | bytes 12544000
  641.1 509.0 %reduce-scatter.11.cloned.1.call-start = ((), (), s32[]{:S(2)}) async-start(), calls=%async_computation.8 | async-start | bytes 12902400 | tf_op jit(solution)/shard_map/reduce_scatter | solution.py:228
  666.9 9.4 slice-start
  666.9 607.8 %all-reduce.17.cloned.1.call-start = ((), (), s32[]{:S(2)}) async-start(), calls=%async_computation.12 | async-start | bytes 15339520 | tf_op jit(solution)/shard_map/psum | solution.py:232
  1150.1 14.9 %copy-start.84 = (f32[128]{0:T(128)S(1)}, f32[128]{0:T(128)}, u32[]{:S(2)}) copy-start(f32[128]{0:T(128)} %get-tuple-element.17) | copy-start | bytes 1540
  1150.1 14.9 %copy-start.83 = (f32[128]{0:T(128)S(1)}, f32[128]{0:T(128)}, u32[]{:S(2)}) copy-start(f32[128]{0:T(128)} %get-tuple-element.18) | copy-start | bytes 1540
  1150.1 14.9 %copy-start.82 = (f32[128]{0:T(128)S(1)}, f32[128]{0:T(128)}, u32[]{:S(2)}) copy-start(f32[128]{0:T(128)} %get-tuple-element.20) | copy-start | bytes 1540
  1150.1 15.0 %copy-start.81 = (f32[128]{0:T(128)S(1)}, f32[128]{0:T(128)}, u32[]{:S(2)}) copy-start(f32[128]{0:T(128)} %get-tuple-element.21) | copy-start | bytes 1540
  1150.1 15.0 %copy-start.11 = (f32[128,1120]{0,1:T(8,128)S(1)}, f32[128,1120]{0,1:T(8,128)}, u32[]{:S(2)}) copy-start(f32[128,1120]{0,1:T(8,128)} %copy-done.8) | copy-start | bytes 1720324
  1150.1 15.0 %copy-start.20 = (f32[128,4480]{1,0:T(8,128)S(1)}, f32[128,4480]{1,0:T(8,128)}, u32[]{:S(2)}) copy-start(f32[128,4480]{1,0:T(8,128)} %fusion.105) | copy-start | bytes 6881284
  1173.5 9.4 copy-start.16
  1173.5 9.4 copy-start.23
  1173.5 9.4 copy-start.25
  1173.5 9.4 copy-start.58
  1173.5 9.4 copy-start.59
  (64 other events, 255.2 us)
Sparse Core Ops, SparseCore 0:
  9.6 141.9 all-gather.4
  153.1 52.2 all-gather.6
  206.9 175.2 all-gather.8
  383.7 179.3 all-gather.10
  593.5 49.2 reduce-scatter.14
  644.9 135.2 reduce-scatter.12
  782.5 185.2 reduce-scatter.16
  970.2 179.8 reduce-scatter.10
  1153.9 120.8 all-reduce.16
where the time goes:
time: 1300 us; the launch traced here: 1290 us
  waiting for transfers between devices  1040 us (80%)
  matrix products  148 us (11%)
  blocking collectives  57.2 us (4%)
  other arithmetic  19.2 us (1%)
  between operations  17 us (1%)
  local copies, waits for them, and re-layouts  13.7 us (1%)
    unnamed x12, waiting for transfers between devices  269 us
    reduce_scatter x1, waiting for transfers between devices, shards(): lax.psum_scatter(grad.astype(jnp.bfloat16), 'narrow', scatter_dimension=0...  182 us
    all_gather x1, waiting for transfers between devices, shards(): lax.all_gather(w_proj, 'narrow', axis=0, tiled=True)  173 us
    all_gather x1, waiting for transfers between devices, shards(): lax.all_gather(w_fc, 'narrow', axis=0, tiled=True)  161 us
    all_gather x1, waiting for transfers between devices, shards(): lax.all_gather(w_qkv, 'narrow', axis=0, tiled=True)  116 us
    psum x1, waiting for transfers between devices, shards(): part = lax.psum(part, 'wide').astype(jnp.float32)  90.5 us
    dot_general x8, matrix products, inner_rows(): lax.dot_general(left, right, (((0,), (0,)), ((), ())), preferred_element_...  64.1 us
    all_gather x1, waiting for transfers between devices, shards(): lax.all_gather(w_out, 'narrow', axis=0, tiled=True)  45.3 us
  transfers between devices with their start and end apart: 9, of which 8 were waited for; matrix products, arithmetic and copies ran while one was open for 10% of the time, Pallas kernels for 0%

commit v1 on v0

--- a/solution.py
+++ b/solution.py
@@ -229,7 +229,7 @@
             grad.astype(jnp.bfloat16), "narrow", scatter_dimension=0, tiled=True
         )
         if part.ndim == 2:
-            part = lax.psum(part, "wide").astype(jnp.float32)
+            part = jnp.sum(lax.all_gather(part, "wide"), axis=0).astype(jnp.float32)
         else:
             part = lax.psum(part.astype(jnp.float32), "wide")
         totals.append(part)

time: 1300 us -> 1520 us (1.17)
  waiting for transfers between devices: 1040 us -> 1220 us
  other arithmetic: 19.2 us -> 56.1 us
    all_gather x0 -> x4, waiting for transfers between devices: none -> 245 us  [shards(): part = jnp.sum(lax.all_gather(part, 'wide'), axis=0).astype(jnp.float32)]
    psum x1 -> x0, waiting for transfers between devices: 90.5 us -> none  [shards(): part = lax.psum(part, 'wide').astype(jnp.float32)]
    reduce_sum x0 -> x4, other arithmetic: none -> 35.3 us  [shards(): part = jnp.sum(lax.all_gather(part, 'wide'), axis=0).astype(jnp.float32)]
    unnamed x12 -> x15, waiting for transfers between devices: 269 us -> 303 us
  transfers between devices with their start and end apart: 9 -> 12, of which waited for: 8 -> 10; matrix products, arithmetic and copies ran while one was open for 10% -> 11% of each run, Pallas kernels for 0% -> 0%
where the time goes in v1:
time: 1520 us; the launch traced here: 1510 us
  waiting for transfers between devices  1220 us (80%)
  matrix products  149 us (10%)
  other arithmetic  56.1 us (4%)
  blocking collectives  53.7 us (4%)
  between operations  16.9 us (1%)
    unnamed x15, waiting for transfers between devices  303 us
    all_gather x4, waiting for transfers between devices, shards(): part = jnp.sum(lax.all_gather(part, 'wide'), axis=0).astype(jnp.float32)  245 us
    reduce_scatter x1, waiting for transfers between devices, shards(): lax.psum_scatter(grad.astype(jnp.bfloat16), 'narrow', scatter_dimension=0...  181 us
    all_gather x1, waiting for transfers between devices, shards(): lax.all_gather(w_proj, 'narrow', axis=0, tiled=True)  173 us
    all_gather x1, waiting for transfers between devices, shards(): lax.all_gather(w_fc, 'narrow', axis=0, tiled=True)  161 us
    all_gather x1, waiting for transfers between devices, shards(): lax.all_gather(w_qkv, 'narrow', axis=0, tiled=True)  116 us
    dot_general x8, matrix products, inner_rows(): lax.dot_general(left, right, (((0,), (0,)), ((), ())), preferred_element_...  64.7 us
    all_gather x1, waiting for transfers between devices, shards(): lax.all_gather(w_out, 'narrow', axis=0, tiled=True)  45.3 us
  transfers between devices with their start and end apart: 12, of which 10 were waited for; matrix products, arithmetic and copies ran while one was open for 11% of the time, Pallas kernels for 0%

profile of v1, /device:TPU:0, one launch (start us, length us, event | category | flops | bytes accessed | tf_op | source)
XLA Modules:
  0.0 1514.1 jit_solution(3001389140364785348)
XLA Ops:
  12.4 21.1 %all-reduce.13 = (bf16[1120]{0:T(1024)(128)(2,1)S(1)}, bf16[1120]{0:T(1024)(128)(2,1)S(1)}, bf16[1120]{0:T(1024)(128)(2,1)S(1)}, bf16[1120]{0:T(1024)(128)(2,1)S(1)}) all-reduce(bf16[1120]{0:T(1024)(128)(2,1)S(1)} %dynamic-update-slice.1, bf16[1120]{0:T(1024)(128)(2,1)S(1)} %dynamic-update-slice, ...), channel_id=1, replica_groups=mesh['wide'=8,'narrow'=4] {'narrow'}, use_global_device_ids=true, to_apply=%add.1 | all-reduce | flops 4480 | bytes 17920
  36.0 115.5 %all-gather.13.cloned.1.call-done = bf16[1120,3360]{1,0:T(8,128)(2,1)} async-done(((bf16[280,3360]{1,0:T(8,128)(2,1)}), bf16[1120,3360]{1,0:T(8,128)(2,1)}) %all-gather.13.cloned.1.call-update) | async-done | bytes 7526416 | tf_op jit(solution)/shard_map/all_gather | solution.py:210
  151.5 6.6 convolution_convert_fusion.1
  160.1 45.3 %all-gather.15.cloned.1.call-done = bf16[1120,1120]{1,0:T(8,128)(2,1)} async-done(((bf16[280,1120]{1,0:T(8,128)(2,1)}), bf16[1120,1120]{1,0:T(8,128)(2,1)}) %all-gather.15.cloned.1.call-update) | async-done | bytes 2508816 | tf_op jit(solution)/shard_map/all_gather | solution.py:211
  208.4 6.6 convolution_convert_fusion
  220.9 161.4 %all-gather.17.cloned.1.call-done = bf16[1120,4480]{1,0:T(8,128)(2,1)} async-done(((bf16[280,4480]{1,0:T(8,128)(2,1)}), bf16[1120,4480]{1,0:T(8,128)(2,1)}) %all-gather.17.cloned.1.call-update) | async-done | bytes 10035216 | tf_op jit(solution)/shard_map/all_gather | solution.py:214
  382.2 7.4 fusion.105
  389.7 173.4 %all-gather.19.cloned.1.call-done = bf16[4480,1120]{1,0:T(8,128)(2,1)} async-done(((bf16[1120,1120]{1,0:T(8,128)(2,1)}), bf16[4480,1120]{1,0:T(8,128)(2,1)}) %all-gather.19.cloned.1.call-update) | async-done | bytes 10035216 | tf_op jit(solution)/shard_map/all_gather | solution.py:215
  563.1 8.1 fusion.21
  577.0 8.1 fusion.14
  585.1 4.0 multiply_reduce_fusion.3
  603.0 7.7 fusion.69
  610.8 8.8 fusion.2
  620.8 9.0 fusion.103
  629.9 11.8 fusion.1
  643.4 9.5 fusion.78
  652.9 14.7 fusion
  668.5 111.2 %reduce-scatter.13.cloned.1.call-done = bf16[280,3360]{1,0:T(8,128)(2,1)} async-done(((bf16[1120,3360]{1,0:T(8,128)(2,1)}), bf16[280,3360]{1,0:T(8,128)(2,1)}) %reduce-scatter.13.cloned.1.call-update) | async-done | bytes 1881616
  779.8 188.9 %reduce-scatter.17.cloned.1.call-done = bf16[280,4480]{1,0:T(8,128)(2,1)} async-done(((bf16[1120,4480]{1,0:T(8,128)(2,1)}), bf16[280,4480]{1,0:T(8,128)(2,1)}) %reduce-scatter.17.cloned.1.call-update) | async-done | bytes 2508816
  968.7 181.0 %reduce-scatter.11.cloned.1.call-done = bf16[1120,1120]{1,0:T(8,128)(2,1)} async-done(((bf16[4480,1120]{1,0:T(8,128)(2,1)}), bf16[1120,1120]{1,0:T(8,128)(2,1)}) %reduce-scatter.11.cloned.1.call-update) | async-done | bytes 2508816 | tf_op jit(solution)/shard_map/reduce_scatter | solution.py:228
  1153.0 5.7 fusion.68
  1158.8 3.7 fusion.66
  1162.5 19.2 %all-reduce.12 = (bf16[1120]{0:T(1024)(128)(2,1)S(1)}, bf16[1120]{0:T(1024)(128)(2,1)S(1)}, bf16[1120]{0:T(1024)(128)(2,1)S(1)}, bf16[1120]{0:T(1024)(128)(2,1)S(1)}) all-reduce(bf16[1120]{0:T(1024)(128)(2,1)S(1)} %add_convert_fusion.5, ...), channel_id=6, replica_groups=mesh['wide'=8,'narrow'=4] {'narrow'}, use_global_device_ids=true, to_apply=%region_24.25.clone | all-reduce | flops 4480 | bytes 17920
  1182.0 13.4 all-reduce.11
  1198.0 9.4 fusion.6
  1207.5 8.2 fusion.7
  1222.6 57.1 %all-gather.21.cloned.1.call-done = bf16[2240,3360]{1,0:T(8,128)(2,1)} async-done(((bf16[280,3360]{1,0:T(8,128)(2,1)}), bf16[2240,3360]{1,0:T(8,128)(2,1)}) %all-gather.21.cloned.1.call-update) | async-done | bytes 15052816 | tf_op jit(solution)/shard_map/all_gather | solution.py:232
  1279.7 8.6 reduce_sum.324
  1290.7 94.6 %all-gather.25.cloned.1.call-done = bf16[2240,4480]{1,0:T(8,128)(2,1)} async-done(((bf16[280,4480]{1,0:T(8,128)(2,1)}), bf16[2240,4480]{1,0:T(8,128)(2,1)}) %all-gather.25.cloned.1.call-update) | async-done | bytes 20070416 | tf_op jit(solution)/shard_map/all_gather | solution.py:232
  1385.3 11.9 reduce_sum.330
  1400.0 93.2 %all-gather.27.cloned.1.call-done = bf16[8960,1120]{1,0:T(8,128)(2,1)} async-done(((bf16[1120,1120]{1,0:T(8,128)(2,1)}), bf16[8960,1120]{1,0:T(8,128)(2,1)}) %all-gather.27.cloned.1.call-update) | async-done | bytes 20070416 | tf_op jit(solution)/shard_map/all_gather | solution.py:232
  1493.1 11.3 reduce_sum.331
  (265 shorter events, 60.9 us)
Async XLA Ops:
  7.2 144.3 %all-gather.13.cloned.1.call-start = ((), (), s32[]{:S(2)}) async-start(), calls=%async_computation.4 | async-start | bytes 9676800 | tf_op jit(solution)/shard_map/all_gather | solution.py:210
  7.9 197.4 %all-gather.15.cloned.1.call-start = ((), (), s32[]{:S(2)}) async-start(), calls=%async_computation.5 | async-start | bytes 3225600 | tf_op jit(solution)/shard_map/all_gather | solution.py:211
  8.7 24.8 %copy-start.71 = (s32[2]{0:T(128)S(1)}, s32[2]{0:T(128)}, u32[]{:S(2)}) copy-start(s32[2]{0:T(128)} %param.12) | copy-start | bytes 28
  8.7 26.7 %copy-start.11 = (bf16[2,128,1120]{1,2,0:T(8,128)(2,1)S(1)}, bf16[2,128,1120]{1,2,0:T(8,128)(2,1)}, u32[]{:S(2)}) copy-start(bf16[2,128,1120]{1,2,0:T(8,128)(2,1)} %param.11) | copy-start | bytes 1720324
  8.7 373.5 %all-gather.17.cloned.1.call-start = ((), (), s32[]{:S(2)}) async-start(), calls=%async_computation.6 | async-start | bytes 12544000 | tf_op jit(solution)/shard_map/all_gather | solution.py:214
  9.5 553.6 %all-gather.19.cloned.1.call-start = ((), (), s32[]{:S(2)}) async-start(), calls=%async_computation.7 | async-start | bytes 12902400 | tf_op jit(solution)/shard_map/all_gather | solution.py:215
  10.0 657.7 %reduce-scatter.15.cloned.1.call-start = ((), (), s32[]{:S(2)}) async-start(), calls=%async_computation.14 | async-start | bytes 3225600
  35.6 172.8 %copy-start.62 = (f32[128]{0:T(128)}, f32[128]{0:T(128)S(1)}, u32[]{:S(2)}) copy-start(f32[128]{0:T(128)S(1)} %get-tuple-element.76) | copy-start | bytes 1540
  35.6 567.3 %copy-start.55 = (f32[128]{0:T(128)}, f32[128]{0:T(128)S(1)}, u32[]{:S(2)}) copy-start(f32[128]{0:T(128)S(1)} %get-tuple-element.77) | copy-start | bytes 1540
  35.8 567.1 %copy-start.58 = (f32[128]{0:T(128)}, f32[128]{0:T(128)S(1)}, u32[]{:S(2)}) copy-start(f32[128]{0:T(128)S(1)} %add_rsqrt_fusion.3) | copy-start | bytes 1540
  35.8 172.6 %copy-start.66 = (f32[128]{0:T(128)}, f32[128]{0:T(128)S(1)}, u32[]{:S(2)}) copy-start(f32[128]{0:T(128)S(1)} %add_rsqrt_fusion.1) | copy-start | bytes 1540
  160.1 48.1 %copy-start.48 = (bf16[20,56,128]{2,1,0:T(8,128)(2,1)}, bf16[20,56,128]{2,1,0:T(8,128)(2,1)S(1)}, u32[]{:S(2)}) copy-start(bf16[20,56,128]{2,1,0:T(8,128)(2,1)S(1)} %convolution_convert_fusion.7) | copy-start | bytes 860164
  208.2 411.5 %copy-start.6 = (f32[128,1120]{0,1:T(8,128)}, f32[128,1120]{0,1:T(8,128)S(1)}, u32[]{:S(2)}) copy-start(f32[128,1120]{0,1:T(8,128)S(1)} %get-tuple-element.69) | copy-start | bytes 1720324
  563.1 9.2 copy-start
  593.4 186.3 %reduce-scatter.13.cloned.1.call-start = ((), (), s32[]{:S(2)}) async-start(), calls=%async_computation.13 | async-start | bytes 9676800
  597.5 13.2 copy-start.35
  597.9 12.9 copy-start.36
  619.6 10.2 copy-start.10
  619.6 349.0 %reduce-scatter.17.cloned.1.call-start = ((), (), s32[]{:S(2)}) async-start(), calls=%async_computation.15 | async-start | bytes 12544000
  641.6 508.0 %reduce-scatter.11.cloned.1.call-start = ((), (), s32[]{:S(2)}) async-start(), calls=%async_computation.8 | async-start | bytes 12902400 | tf_op jit(solution)/shard_map/reduce_scatter | solution.py:228
  667.7 550.3 %all-gather.23.cloned.1.call-start = ((), (), s32[]{:S(2)}) async-start(), calls=%async_computation.10 | async-start | bytes 5806080 | tf_op jit(solution)/shard_map/all_gather | solution.py:232
  668.4 611.3 %all-gather.21.cloned.1.call-start = ((), (), s32[]{:S(2)}) async-start(), calls=%async_computation.9 | async-start | bytes 17418240 | tf_op jit(solution)/shard_map/all_gather | solution.py:232
  779.7 605.6 %all-gather.25.cloned.1.call-start = ((), (), s32[]{:S(2)}) async-start(), calls=%async_computation.11 | async-start | bytes 22579200 | tf_op jit(solution)/shard_map/all_gather | solution.py:232
  968.6 190.1 %slice-start = ((s8[7741440]{0:T(1024)(128)(4,1)}), s8[3547136]{0:T(1024)(128)(4,1)S(1)}, s32[]{:S(2)}) async-start(s8[7741440]{0:T(1024)(128)(4,1)} %bitcast.188), calls=%async_computation.16 | async-start | bytes 7094272
  968.7 524.5 %all-gather.27.cloned.1.call-start = ((), (), s32[]{:S(2)}) async-start(), calls=%async_computation.12 | async-start | bytes 23224320 | tf_op jit(solution)/shard_map/all_gather | solution.py:232
  1198.0 9.4 copy-start.7
  1198.0 9.5 copy-start.18
  1207.4 9.2 copy-start.15
  1207.5 9.2 copy-start.21
  1207.5 9.2 copy-start.23
  1207.5 9.2 copy-start.53
  1207.5 9.1 copy-start.54
  (58 other events, 220.6 us)
Sparse Core Ops, SparseCore 0:
  9.6 141.9 all-gather.12
  153.1 52.2 all-gather.14
  206.9 175.2 all-gather.16
  383.7 179.3 all-gather.18
  593.5 49.2 reduce-scatter.14
  644.9 134.7 reduce-scatter.12
  782.1 186.5 reduce-scatter.16
  971.0 178.6 reduce-scatter.10
  1151.6 41.8 all-gather.22
  1195.2 84.4 all-gather.20
  1281.6 103.6 all-gather.24
  1387.0 106.0 all-gather.26
